TPU v7x, 32 devices: a whole 2x2x4 slice. The times are simulated.
32 devices in a mesh: clip: 2 (over core), tm: 16 (over z, y, x).
Axes of the slice: x: 2, y: 2, z: 4, core: 2. Of those that a mesh axis runs over, the one named last changes fastest.
Arguments:
- clip_frames: bfloat16 [2, 32, 64, 64, 128], P('clip', 'tm'), may hold values from -6 to 6
- spatial_weight: bfloat16 [3, 3, 128, 256], replicated, may hold values from -0.1875 to 0.1875
- norm_gain: float32 [256], replicated, may hold values from 0.5 to 1.5
- norm_bias: float32 [256], replicated, may hold values from -3 to 3
- temporal_weight: bfloat16 [3, 256, 256], replicated, may hold values from -0.21875 to 0.21875
- cotangent: bfloat16 [2, 32, 32, 32, 256], P('clip', 'tm'), may hold values from -0.0234375 to 0.0234375
Outputs:
- mixed: bfloat16 [2, 32, 32, 32, 256], P('clip', 'tm')
- spatial_grad: float32 [3, 3, 128, 256], replicated
- gain_grad: float32 [256], replicated
- bias_grad: float32 [256], replicated
- temporal_grad: float32 [3, 256, 256], replicated
All inputs are finite; a program needn't handle non-finite values.
Results may differ from a plain program's by a relative error of at most 0.0085.
Values may be sent and summed in bfloat16 or wider, within the bound.
A program may use at most 64 MiB of HBM per device.

v0:
```python
import jax
import jax.numpy as jnp
from jax import lax
from jax.sharding import PartitionSpec as P

GROUPS = 32
DILATION_FRAMES = 4
epsilon = 1e-05


def delay_rows(values):
    return jnp.pad(values, ((0, 0), (1, 0), (0, 0), (0, 0)))[:, :-1]


def delay_cols(values):
    return jnp.pad(values, ((0, 0), (0, 0), (1, 0), (0, 0)))[:, :, :-1]


def advance_rows(values):
    return jnp.pad(values, ((0, 0), (0, 1), (0, 0), (0, 0)))[:, 1:]


def advance_cols(values):
    return jnp.pad(values, ((0, 0), (0, 0), (0, 1), (0, 0)))[:, :, 1:]


def split_phases(frames_in):
    frames, height, width, chans = frames_in.shape
    viewed = frames_in.reshape(frames, height // 2, 2, width // 2, 2, chans)
    phases = {}
    for row_phase in range(2):
        for col_phase in range(2):
            phases[row_phase, col_phase] = viewed[:, :, row_phase, :, col_phase, :].reshape(
                -1, chans
            )
    return phases


def tap_layout(offset):
    return (0 if offset == 1 else 1, offset == 0)


def membership(chans):
    channel_group = lax.broadcasted_iota(jnp.int32, (chans, GROUPS), 0) // (chans // GROUPS)
    group_index = lax.broadcasted_iota(jnp.int32, (chans, GROUPS), 1)
    return (channel_group == group_index).astype(jnp.float32)


def activate(conv_out, gain, bias):
    chans = conv_out.shape[-1]
    member = membership(chans)
    count = conv_out.shape[1] * conv_out.shape[2] * (chans // GROUPS)
    high = lax.Precision.HIGHEST
    chan_sum = jnp.sum(conv_out, axis=(1, 2))
    group_mean = jnp.dot(chan_sum, member, precision=high) / count
    center = jnp.dot(group_mean, member.T, precision=high)
    deviation = conv_out - center[:, None, None, :]
    chan_square = jnp.sum(deviation * deviation, axis=(1, 2))
    group_var = jnp.dot(chan_square, member, precision=high) / count
    scaling = jnp.dot(lax.rsqrt(group_var + epsilon), member.T, precision=high)
    normed = deviation * scaling[:, None, None, :]
    return jax.nn.silu(normed * gain + bias)


def padded_lag(values, frame_offset):
    if frame_offset == 0:
        return values
    frames = values.shape[0]
    if frame_offset > 0:
        filler = jnp.zeros((frame_offset,) + values.shape[1:], values.dtype)
        return jnp.concatenate([filler, values[: frames - frame_offset]], axis=0)
    filler = jnp.zeros((-frame_offset,) + values.shape[1:], values.dtype)
    return jnp.concatenate([values[-frame_offset:], filler], axis=0)


def temporal_pass(acts, grads, weight, lag_rule):
    chans = acts.shape[-1]
    total = acts.astype(jnp.float32)
    backward_total_sum = grads.astype(jnp.float32)
    tap_grads = []
    flattened_gradients = grads.reshape(-1, chans)
    for kernel_tap_index in range(3):
        frame_offset = kernel_tap_index * DILATION_FRAMES
        earlier = lag_rule(acts, frame_offset).reshape(-1, chans)
        later = lag_rule(grads, -frame_offset).reshape(-1, chans)
        total = total + jnp.dot(
            earlier, weight[kernel_tap_index], preferred_element_type=jnp.float32
        ).reshape(acts.shape)
        backward_total_sum = backward_total_sum + jnp.dot(
            later, weight[kernel_tap_index].T, preferred_element_type=jnp.float32
        ).reshape(acts.shape)
        tap_grads.append(
            lax.dot_general(
                earlier,
                flattened_gradients,
                (((0,), (0,)), ((), ())),
                preferred_element_type=jnp.float32,
            )
        )
    return (
        total.astype(jnp.bfloat16),
        backward_total_sum.astype(jnp.bfloat16),
        jnp.stack(tap_grads),
    )


def per_device(clip_frames, spatial_weight, norm_gain, norm_bias, temporal_weight, cotangent):
    frames_in = clip_frames[0]
    upstream = cotangent[0]
    frames, height, width, _ = frames_in.shape
    out_chans = spatial_weight.shape[-1]
    out_shape = (frames, height // 2, width // 2, out_chans)
    phases = split_phases(frames_in)
    partial_sums = {}
    for row_offset in range(3):
        row_phase, row_delay = tap_layout(row_offset)
        for col_offset in range(3):
            col_phase, col_delay = tap_layout(col_offset)
            product = jnp.dot(
                phases[row_phase, col_phase],
                spatial_weight[row_offset, col_offset],
                preferred_element_type=jnp.float32,
            )
            key_pair = (row_delay, col_delay)
            if key_pair in partial_sums:
                partial_sums[key_pair] = partial_sums[key_pair] + product
            else:
                partial_sums[key_pair] = product
    conv_out = partial_sums[False, False].reshape(out_shape)
    conv_out = conv_out + delay_rows(partial_sums[True, False].reshape(out_shape))
    conv_out = conv_out + delay_cols(partial_sums[False, True].reshape(out_shape))
    conv_out = conv_out + delay_rows(delay_cols(partial_sums[True, True].reshape(out_shape)))
    activated, pullback = jax.vjp(activate, conv_out, norm_gain, norm_bias)
    acts = activated.astype(jnp.bfloat16)
    act_rows = lax.all_to_all(acts, "tm", split_axis=1, concat_axis=0, tiled=True)
    grad_rows = lax.all_to_all(upstream, "tm", split_axis=1, concat_axis=0, tiled=True)
    mixed_rows, act_grad_rows, temporal_part = temporal_pass(
        act_rows, grad_rows, temporal_weight, padded_lag
    )
    mixed = lax.all_to_all(mixed_rows, "tm", split_axis=0, concat_axis=1, tiled=True)
    act_grad = lax.all_to_all(act_grad_rows, "tm", split_axis=0, concat_axis=1, tiled=True)
    conv_grad, gain_partial_sum, bias_part = pullback(act_grad.astype(jnp.float32))
    conv_grad = conv_grad.astype(jnp.bfloat16)
    grad_versions = {
        (False, False): conv_grad.reshape(-1, out_chans),
        (True, False): advance_rows(conv_grad).reshape(-1, out_chans),
        (False, True): advance_cols(conv_grad).reshape(-1, out_chans),
        (True, True): advance_rows(advance_cols(conv_grad)).reshape(-1, out_chans),
    }
    tap_rows = []
    for row_offset in range(3):
        row_phase, row_delay = tap_layout(row_offset)
        tap_row = []
        for col_offset in range(3):
            col_phase, col_delay = tap_layout(col_offset)
            tap_row.append(
                lax.dot_general(
                    phases[row_phase, col_phase],
                    grad_versions[row_delay, col_delay],
                    (((0,), (0,)), ((), ())),
                    preferred_element_type=jnp.float32,
                )
            )
        tap_rows.append(jnp.stack(tap_row))
    spatial_part = jnp.stack(tap_rows)
    spatial_gradient_total, gain_total, bias_total, temporal_total = lax.psum(
        (spatial_part, gain_partial_sum, bias_part, temporal_part), ("clip", "tm")
    )
    return (mixed[None], spatial_gradient_total, gain_total, bias_total, temporal_total)


def solution(mesh):
    return jax.shard_map(
        per_device,
        mesh=mesh,
        in_specs=(
            P("clip", "tm", None, None, None),
            P(),
            P(),
            P(),
            P(),
            P("clip", "tm", None, None, None),
        ),
        out_specs=(P("clip", "tm", None, None, None), P(), P(), P(), P()),
        check_vma=False,
    )
```

profile of v0, /device:TPU:0, one launch (start us, length us, event | category | flops | bytes accessed | tf_op | source)
XLA Modules:
  0.0 279.1 jit_solution(15549774472298984337)
XLA Ops:
  7.2 2.4 copy.71
  9.6 8.4 %all-to-all-start.2 = ((bf16[2,32,32,256]{3,2,0,1:T(8,128)(2,1)}), bf16[2,32,32,256]{3,2,0,1:T(8,128)(2,1)}, u32[]{:S(2)}, u32[]{:S(2)}) async-start(bf16[2,32,32,256]{3,2,0,1:T(8,128)(2,1)} %bitcast.205), calls=%async_computation.2 | async-start | bytes 2097152 | tf_op jit(solution)/shard_map/all_to_all | solution.py:136
  18.0 4.5 %fusion.86 = (bf16[2,32,1,32,1,128]{5,4,3,2,1,0:T(2,128)(2,1)S(1)}, bf16[2,32,1,32,1,128]{5,4,3,2,1,0:T(2,128)(2,1)S(1)}, bf16[2,32,1,32,1,128]{5,4,3,2,1,0:T(2,128)(2,1)S(1)}, bf16[2,32,1,32,1,128]{5,4,3,2,1,0:T(2,128)(2,1)S(1)}) fusion(bf16[2,32,2,32,2,128]{5,4,3,2,1,0:T(2,128)(2,1)S(1)} %bitcast.240), kind=kLoop, calls=%fused_computation.138 | loop fusion | bytes 4194304 | tf_op jit(solution)/shard_map/slice | solution.py:33
  24.1 1.8 fusion.32
  25.9 1.8 fusion.7
  28.1 1.8 convolution_add_fusion.3
  29.9 1.7 convolution_add_fusion.1
  31.6 10.9 %all-to-all-done.2 = bf16[2,32,32,256]{3,2,0,1:T(8,128)(2,1)} async-done(((bf16[2,32,32,256]{3,2,0,1:T(8,128)(2,1)}), bf16[2,32,32,256]{3,2,0,1:T(8,128)(2,1)}, u32[]{:S(2)}, u32[]{:S(2)}) %all-to-all-start.2) | async-done | bytes 1048608 | tf_op jit(solution)/shard_map/all_to_all | solution.py:136
  45.7 1.6 add_convert_fusion.1
  47.3 5.9 %all-to-all-start.3 = ((bf16[32,2,32,256]{3,2,1,0:T(8,128)(2,1)}), bf16[32,2,32,256]{3,2,1,0:T(8,128)(2,1)}, u32[]{:S(2)}, u32[]{:S(2)}) async-start(bf16[32,2,32,256]{3,2,1,0:T(8,128)(2,1)} %add_convert_fusion.1), calls=%async_computation.3 | async-start | bytes 2097152 | tf_op jit(solution)/shard_map/all_to_all | solution.py:141
  53.2 2.1 pad_slice_fusion
  57.7 1.8 fusion.84
  62.0 14.2 %all-to-all-done.3 = bf16[32,2,32,256]{3,2,1,0:T(8,128)(2,1)} async-done(((bf16[32,2,32,256]{3,2,1,0:T(8,128)(2,1)}), bf16[32,2,32,256]{3,2,1,0:T(8,128)(2,1)}, u32[]{:S(2)}, u32[]{:S(2)}) %all-to-all-start.3) | async-done | bytes 1048608 | tf_op jit(solution)/shard_map/all_to_all | solution.py:141
  77.8 3.2 %fusion.82 = (f32[256]{0:T(256)}, f32[2,256]{1,0:T(2,128)S(1)}, f32[2,32,32,256]{3,2,1,0:T(8,128)}, bf16[2,32,32,256]{3,2,1,0:T(8,128)(2,1)S(1)}) fusion(f32[256]{0:T(256)S(1)} %copy-done.17, f32[2,32,32,256]{3,2,1,0:T(8,128)S(1)} %get-tuple-element.40, f32[2,256]{1,0:T(2,128)S(1)} %fusion.23, f32[2,32,32,256]{3,2,1,0:T(8,128)S(1)} %bitcast.239, ...), kind=kLoop, calls=%fused_computation.136 | loop fusion | flops 9960704 | bytes 7349248 | tf_op jit(solution)/shard_map/transpose(jvp())/reduce_sum | solution.py:62
  82.7 6.1 %all-to-all-start = ((bf16[2,32,32,256]{3,2,0,1:T(8,128)(2,1)}), bf16[2,32,32,256]{3,2,0,1:T(8,128)(2,1)}, u32[]{:S(2)}, u32[]{:S(2)}) async-start(bf16[2,32,32,256]{3,2,0,1:T(8,128)(2,1)} %copy.36), calls=%async_computation | async-start | bytes 2097152 | tf_op jit(solution)/shard_map/all_to_all | solution.py:135
  88.8 2.9 %multiply_reduce_fusion = (f32[256]{0:T(256)}, f32[2,256]{1,0:T(2,128)S(1)}) fusion(f32[2,32,32,256]{3,2,1,0:T(8,128)} %get-tuple-element.38, f32[2,32,32,256]{3,2,1,0:T(8,128)S(1)} %get-tuple-element.40, f32[2,256]{1,0:T(2,128)S(1)} %fusion.22, f32[2,256]{1,0:T(2,128)S(1)} %fusion.23, f32[2,256]{1,0:T(2,128)S(1)} %fusion.21, f32[256]{0:T(256)S(1)} %copy-done.17), kind=kLoop, calls=%fused_computation.16 | loop fusion | flops 5242112 | bytes 4204544 | tf_op jit(solution)/shard_map/transpose(jvp())/reduce_sum | solution.py:62
  100.4 11.3 %all-to-all-done = bf16[2,32,32,256]{3,2,0,1:T(8,128)(2,1)} async-done(((bf16[2,32,32,256]{3,2,0,1:T(8,128)(2,1)}), bf16[2,32,32,256]{3,2,0,1:T(8,128)(2,1)}, u32[]{:S(2)}, u32[]{:S(2)}) %all-to-all-start) | async-done | bytes 1048608 | tf_op jit(solution)/shard_map/all_to_all | solution.py:135
  115.5 6.2 %all-to-all-start.1 = ((bf16[32,2,32,256]{3,2,1,0:T(8,128)(2,1)}), bf16[32,2,32,256]{3,2,1,0:T(8,128)(2,1)}, u32[]{:S(2)}, u32[]{:S(2)}) async-start(bf16[32,2,32,256]{3,2,1,0:T(8,128)(2,1)} %add_convert_fusion.2), calls=%async_computation.1 | async-start | bytes 2097152 | tf_op jit(solution)/shard_map/all_to_all | solution.py:140
  121.7 2.1 pad_maximum_fusion
  125.0 2.0 convolution_bitcast_fusion.2
  128.1 43.7 %all-reduce.11 = (f32[256]{0:T(256)}, f32[256]{0:T(256)}) all-reduce(f32[256]{0:T(256)S(1)} %copy-done.19, f32[256]{0:T(256)S(1)} %copy-done.18), channel_id=1, replica_groups=mesh['clip'=2,'tm'=16] {'clip','tm'}, use_global_device_ids=true, to_apply=%region_6.7 | all-reduce | flops 512 | bytes 4096 | tf_op jit(solution)/shard_map/psum | solution.py:166
  171.7 94.6 %all-reduce.15.cloned.1.call-done = (f32[3,3,128,256]{2,3,1,0:T(8,128)}, f32[3,256,256]{2,1,0:T(8,128)}) async-done(((f32[3,3,128,256]{2,3,1,0:T(8,128)}, f32[3,256,256]{2,1,0:T(8,128)}), (f32[3,3,128,256]{2,3,1,0:T(8,128)}, f32[3,256,256]{2,1,0:T(8,128)})) %all-reduce.15.cloned.1.call-update) | async-done | bytes 1966096 | tf_op jit(solution)/shard_map/psum | solution.py:166
  266.4 2.7 copy.44
  269.1 2.3 copy.39
  (124 shorter events, 28.7 us)
Async XLA Ops:
  7.2 10.8 %copy-start.8 = (bf16[1,2,64,64,128]{4,3,2,1,0:T(8,128)(2,1)S(1)}, bf16[1,2,64,64,128]{4,3,2,1,0:T(8,128)(2,1)}, u32[]{:S(2)}) copy-start(bf16[1,2,64,64,128]{4,3,2,1,0:T(8,128)(2,1)} %param.6) | copy-start | bytes 6291460
  9.6 32.9 %all-to-all-start.2 = ((bf16[2,32,32,256]{3,2,0,1:T(8,128)(2,1)}), bf16[2,32,32,256]{3,2,0,1:T(8,128)(2,1)}, u32[]{:S(2)}, u32[]{:S(2)}) async-start(bf16[2,32,32,256]{3,2,0,1:T(8,128)(2,1)} %bitcast.205), calls=%async_computation.2 | async-start | bytes 2097152 | tf_op jit(solution)/shard_map/all_to_all | solution.py:136
  18.0 4.6 %copy-start.16 = (bf16[3,3,128,256]{3,2,1,0:T(8,128)(2,1)S(1)}, bf16[3,3,128,256]{3,2,1,0:T(8,128)(2,1)}, u32[]{:S(2)}) copy-start(bf16[3,3,128,256]{3,2,1,0:T(8,128)(2,1)} %param.7) | copy-start | bytes 1769476
  23.4 36.4 %copy-start.21 = (s32[256]{0:T(256)}, s32[256]{0:T(256)S(1)}, u32[]{:S(2)}) copy-start(s32[256]{0:T(256)S(1)} %get-tuple-element.52) | copy-start | bytes 3076
  23.4 36.4 %copy-start.25 = (s32[256]{0:T(256)}, s32[256]{0:T(256)S(1)}, u32[]{:S(2)}) copy-start(s32[256]{0:T(256)S(1)} %get-tuple-element.53) | copy-start | bytes 3076
  23.5 4.2 %copy-start.5 = (bf16[2,32,1,32,1,128]{5,3,4,2,1,0:T(8,128)(2,1)}, bf16[2,32,1,32,1,128]{5,3,4,2,1,0:T(8,128)(2,1)S(1)}, u32[]{:S(2)}) copy-start(bf16[2,32,1,32,1,128]{5,3,4,2,1,0:T(8,128)(2,1)S(1)} %copy.55) | copy-start | bytes 1572868
  23.6 4.6 %copy-start.3 = (bf16[2,32,1,32,1,128]{5,3,4,2,1,0:T(8,128)(2,1)}, bf16[2,32,1,32,1,128]{5,3,4,2,1,0:T(8,128)(2,1)S(1)}, u32[]{:S(2)}) copy-start(bf16[2,32,1,32,1,128]{5,3,4,2,1,0:T(8,128)(2,1)S(1)} %copy.56) | copy-start | bytes 1572868
  23.7 31.6 %copy-start = (bf16[2,32,1,32,1,128]{5,3,1,0,4,2:T(8,128)(2,1)}, bf16[2,32,1,32,1,128]{5,3,1,0,4,2:T(8,128)(2,1)S(1)}, u32[]{:S(2)}) copy-start(bf16[2,32,1,32,1,128]{5,3,1,0,4,2:T(8,128)(2,1)S(1)} %copy.57) | copy-start | bytes 1572868
  47.3 28.9 %all-to-all-start.3 = ((bf16[32,2,32,256]{3,2,1,0:T(8,128)(2,1)}), bf16[32,2,32,256]{3,2,1,0:T(8,128)(2,1)}, u32[]{:S(2)}, u32[]{:S(2)}) async-start(bf16[32,2,32,256]{3,2,1,0:T(8,128)(2,1)} %add_convert_fusion.1), calls=%async_computation.3 | async-start | bytes 2097152 | tf_op jit(solution)/shard_map/all_to_all | solution.py:141
  53.2 7.9 %copy-start.29 = (pred[256]{0:T(512)(128)(4,1)}, pred[256]{0:T(512)(128)(4,1)S(1)}, u32[]{:S(2)}) copy-start(pred[256]{0:T(512)(128)(4,1)S(1)} %compare_and_fusion) | copy-start | bytes 772
  60.8 16.9 %copy-start.17 = (f32[256]{0:T(256)S(1)}, f32[256]{0:T(256)}, u32[]{:S(2)}) copy-start(f32[256]{0:T(256)} %param.8) | copy-start | bytes 3076
  60.8 16.9 %copy-start.20 = (f32[256]{0:T(256)S(1)}, f32[256]{0:T(256)}, u32[]{:S(2)}) copy-start(f32[256]{0:T(256)} %param.9) | copy-start | bytes 3076
  77.7 3.3 %copy-start.23 = (s32[256]{0:T(256)S(1)}, s32[256]{0:T(256)}, u32[]{:S(2)}) copy-start(s32[256]{0:T(256)} %copy-done.21) | copy-start | bytes 3076
  77.7 3.3 %copy-start.27 = (s32[256]{0:T(256)S(1)}, s32[256]{0:T(256)}, u32[]{:S(2)}) copy-start(s32[256]{0:T(256)} %copy-done.25) | copy-start | bytes 3076
  77.7 3.3 %copy-start.30 = (pred[256]{0:T(512)(128)(4,1)S(1)}, pred[256]{0:T(512)(128)(4,1)}, u32[]{:S(2)}) copy-start(pred[256]{0:T(512)(128)(4,1)} %copy-done.29) | copy-start | bytes 772
  77.7 3.3 %copy-start.33 = (f32[2,32]{1,0:T(2,128)S(1)}, f32[2,32]{1,0:T(2,128)}, u32[]{:S(2)}) copy-start(f32[2,32]{1,0:T(2,128)} %copy-done.32) | copy-start | bytes 772
  82.7 28.9 %all-to-all-start = ((bf16[2,32,32,256]{3,2,0,1:T(8,128)(2,1)}), bf16[2,32,32,256]{3,2,0,1:T(8,128)(2,1)}, u32[]{:S(2)}, u32[]{:S(2)}) async-start(bf16[2,32,32,256]{3,2,0,1:T(8,128)(2,1)} %copy.36), calls=%async_computation | async-start | bytes 2097152 | tf_op jit(solution)/shard_map/all_to_all | solution.py:135
  88.8 3.0 %copy-start.24 = (s32[256]{0:T(256)S(1)}, s32[256]{0:T(256)}, u32[]{:S(2)}) copy-start(s32[256]{0:T(256)} %copy-done.21) | copy-start | bytes 3076
  88.8 3.0 %copy-start.28 = (s32[256]{0:T(256)S(1)}, s32[256]{0:T(256)}, u32[]{:S(2)}) copy-start(s32[256]{0:T(256)} %copy-done.25) | copy-start | bytes 3076
  88.8 3.5 %copy-start.2 = (f32[2,32,32,256]{3,2,1,0:T(8,128)S(1)}, f32[2,32,32,256]{3,2,1,0:T(8,128)}, u32[]{:S(2)}) copy-start(f32[2,32,32,256]{3,2,1,0:T(8,128)} %get-tuple-element.38) | copy-start | bytes 6291460
  115.5 6.3 %copy-start.14 = (f32[1,3,128,256]{2,3,1,0:T(8,128)S(1)}, f32[1,3,128,256]{2,3,1,0:T(8,128)}, u32[]{:S(2)}) copy-start(f32[1,3,128,256]{2,3,1,0:T(8,128)} %maximum_bitcast_fusion.1) | copy-start | bytes 1179652
  115.5 153.6 %all-to-all-start.1 = ((bf16[32,2,32,256]{3,2,1,0:T(8,128)(2,1)}), bf16[32,2,32,256]{3,2,1,0:T(8,128)(2,1)}, u32[]{:S(2)}, u32[]{:S(2)}) async-start(bf16[32,2,32,256]{3,2,1,0:T(8,128)(2,1)} %add_convert_fusion.2), calls=%async_computation.1 | async-start | bytes 2097152 | tf_op jit(solution)/shard_map/all_to_all | solution.py:140
  121.7 144.7 %all-reduce.15.cloned.1.call-start = ((), (), s32[]{:S(2)}) async-start(), calls=%async_computation.4 | async-start | bytes 3932160 | tf_op jit(solution)/shard_map/psum | solution.py:166
  266.4 5.0 %copy-start.15 = (f32[3,256,256]{2,1,0:T(8,128)S(1)}, f32[3,256,256]{2,1,0:T(8,128)}, u32[]{:S(2)}) copy-start(f32[3,256,256]{2,1,0:T(8,128)} %get-tuple-element.58) | copy-start | bytes 2359300
  (15 other events, 19.2 us)
Sparse Core Ops, SparseCore 0:
  128.5 137.7 all-reduce.14
where the time goes:
time: 280 us; the launch traced here: 279 us
  waiting for transfers between devices  131 us (47%)
  blocking collectives  43.7 us (16%)
  starting transfers between devices  26.6 us (10%)
  matrix products  25.9 us (9%)
  local copies, waits for them, and re-layouts  25.6 us (9%)
  between operations  14.6 us (5%)
  other arithmetic  11.8 us (4%)
    psum x1, waiting for transfers between devices, per_device(): lax.psum((spatial_part, gain_partial_sum, bias_part, temporal_part), ('cl...  94.6 us
    psum x1, blocking collectives, per_device(): lax.psum((spatial_part, gain_partial_sum, bias_part, temporal_part), ('cl...  43.7 us
    all_to_all x1, waiting for transfers between devices, per_device(): lax.all_to_all(act_grad_rows, 'tm', split_axis=0, concat_axis=1, tiled=True)  14.2 us
    dot_general x9, matrix products, per_device(): jnp.dot(phases[row_phase, col_phase], spatial_weight[row_offset, col_offs...  11.5 us
    all_to_all x1, waiting for transfers between devices, per_device(): lax.all_to_all(acts, 'tm', split_axis=1, concat_axis=0, tiled=True)  11.3 us
    all_to_all x1, waiting for transfers between devices, per_device(): lax.all_to_all(upstream, 'tm', split_axis=1, concat_axis=0, tiled=True)  10.9 us
    unnamed x75, local copies, waits for them, and re-layouts  10.3 us
    all_to_all x1, starting transfers between devices, per_device(): lax.all_to_all(upstream, 'tm', split_axis=1, concat_axis=0, tiled=True)  8.36 us
  transfers between devices with their start and end apart: 5, of which 4 were waited for; matrix products, arithmetic and copies ran while one was open for 14% of the time, Pallas kernels for 0%

commit v1 on v0

--- a/solution.py
+++ b/solution.py
@@ -2,6 +2,7 @@
 import jax.numpy as jnp
 from jax import lax
 from jax.sharding import PartitionSpec as P
+from jax.lax import all_to_all, axis_size
 
 GROUPS = 32
 DILATION_FRAMES = 4
@@ -138,7 +139,9 @@
         act_rows, grad_rows, temporal_weight, padded_lag
     )
     mixed = lax.all_to_all(mixed_rows, "tm", split_axis=0, concat_axis=1, tiled=True)
-    act_grad = lax.all_to_all(act_grad_rows, "tm", split_axis=0, concat_axis=1, tiled=True)
+    act_grad = jnp.concatenate(
+        all_to_all(jnp.stack(jnp.split(act_grad_rows, axis_size("tm"), axis=0)), "tm", 0, 0), axis=1
+    )
     conv_grad, gain_partial_sum, bias_part = pullback(act_grad.astype(jnp.float32))
     conv_grad = conv_grad.astype(jnp.bfloat16)
     grad_versions = {

time: 280 us -> 290 us (1.036)
  local copies, waits for them, and re-layouts: 25.6 us -> 34.4 us
    unnamed x75 -> x84, local copies, waits for them, and re-layouts: 10.3 us -> 19.8 us
where the time goes in v1:
time: 290 us; the launch traced here: 289 us
  waiting for transfers between devices  131 us (45%)
  blocking collectives  43.5 us (15%)
  local copies, waits for them, and re-layouts  34.4 us (12%)
  starting transfers between devices  26.6 us (9%)
  matrix products  25.6 us (9%)
  between operations  14.6 us (5%)
  other arithmetic  13.4 us (5%)
    psum x1, waiting for transfers between devices, per_device(): lax.psum((spatial_part, gain_partial_sum, bias_part, temporal_part), ('cl...  94.6 us
    psum x1, blocking collectives, per_device(): lax.psum((spatial_part, gain_partial_sum, bias_part, temporal_part), ('cl...  43.5 us
    unnamed x84, local copies, waits for them, and re-layouts  19.8 us
    all_to_all x1, waiting for transfers between devices, per_device(): all_to_all(jnp.stack(jnp.split(act_grad_rows, axis_size('tm'), axis=0)),...  14.7 us
    dot_general x9, matrix products, per_device(): jnp.dot(phases[row_phase, col_phase], spatial_weight[row_offset, col_offs...  11.5 us
    all_to_all x1, waiting for transfers between devices, per_device(): lax.all_to_all(acts, 'tm', split_axis=1, concat_axis=0, tiled=True)  11.2 us
    all_to_all x1, waiting for transfers between devices, per_device(): lax.all_to_all(upstream, 'tm', split_axis=1, concat_axis=0, tiled=True)  10.9 us
    all_to_all x1, starting transfers between devices, per_device(): lax.all_to_all(upstream, 'tm', split_axis=1, concat_axis=0, tiled=True)  8.36 us
  transfers between devices with their start and end apart: 5, of which 4 were waited for; matrix products, arithmetic and copies ran while one was open for 14% of the time, Pallas kernels for 0%

profile of v1, /device:TPU:0, one launch (start us, length us, event | category | flops | bytes accessed | tf_op | source)
XLA Modules:
  0.0 289.5 jit_solution(6303809094886744038)
XLA Ops:
  7.2 2.4 copy.71
  9.6 8.4 %all-to-all-start.2 = ((bf16[2,32,32,256]{3,2,0,1:T(8,128)(2,1)}), bf16[2,32,32,256]{3,2,0,1:T(8,128)(2,1)}, u32[]{:S(2)}, u32[]{:S(2)}) async-start(bf16[2,32,32,256]{3,2,0,1:T(8,128)(2,1)} %bitcast.267), calls=%async_computation.2 | async-start | bytes 2097152 | tf_op jit(solution)/shard_map/all_to_all | solution.py:137
  18.0 4.5 %fusion.102 = (bf16[2,32,1,32,1,128]{5,4,3,2,1,0:T(2,128)(2,1)S(1)}, bf16[2,32,1,32,1,128]{5,4,3,2,1,0:T(2,128)(2,1)S(1)}, bf16[2,32,1,32,1,128]{5,4,3,2,1,0:T(2,128)(2,1)S(1)}, bf16[2,32,1,32,1,128]{5,4,3,2,1,0:T(2,128)(2,1)S(1)}) fusion(bf16[2,32,2,32,2,128]{5,4,3,2,1,0:T(2,128)(2,1)S(1)} %bitcast.302), kind=kLoop, calls=%fused_computation.171 | loop fusion | bytes 4194304 | tf_op jit(solution)/shard_map/slice | solution.py:34
  24.1 1.7 fusion.48
  25.9 1.8 fusion.7
  28.1 1.8 convolution_add_fusion.3
  29.9 1.7 convolution_add_fusion.1
  31.6 10.9 %all-to-all-done.2 = bf16[2,32,32,256]{3,2,0,1:T(8,128)(2,1)} async-done(((bf16[2,32,32,256]{3,2,0,1:T(8,128)(2,1)}), bf16[2,32,32,256]{3,2,0,1:T(8,128)(2,1)}, u32[]{:S(2)}, u32[]{:S(2)}) %all-to-all-start.2) | async-done | bytes 1048608 | tf_op jit(solution)/shard_map/all_to_all | solution.py:137
  56.5 5.9 %all-to-all-start.3 = ((bf16[16,2,2,32,256]{4,3,2,1,0:T(8,128)(2,1)}), bf16[16,2,2,32,256]{4,3,2,1,0:T(8,128)(2,1)}, u32[]{:S(2)}, u32[]{:S(2)}) async-start(bf16[16,2,2,32,256]{4,3,2,1,0:T(8,128)(2,1)} %fusion.30), calls=%async_computation.3 | async-start | bytes 2097152 | tf_op jit(solution)/shard_map/all_to_all | solution.py:143
  62.4 2.1 pad_slice_fusion
  66.9 1.8 fusion.100
  70.7 14.7 %all-to-all-done.3 = bf16[16,2,2,32,256]{4,3,2,1,0:T(8,128)(2,1)} async-done(((bf16[16,2,2,32,256]{4,3,2,1,0:T(8,128)(2,1)}), bf16[16,2,2,32,256]{4,3,2,1,0:T(8,128)(2,1)}, u32[]{:S(2)}, u32[]{:S(2)}) %all-to-all-start.3) | async-done | bytes 1048608 | tf_op jit(solution)/shard_map/all_to_all | solution.py:143
  87.6 3.2 %fusion.98 = (f32[256]{0:T(256)}, f32[2,256]{1,0:T(2,128)S(1)}, f32[2,32,32,256]{3,2,1,0:T(8,128)}, bf16[2,32,32,256]{3,2,1,0:T(8,128)(2,1)S(1)}) fusion(f32[256]{0:T(256)S(1)} %copy-done.17, f32[2,32,32,256]{3,2,1,0:T(8,128)S(1)} %get-tuple-element.40, f32[2,256]{1,0:T(2,128)S(1)} %fusion.23, f32[2,32,32,256]{3,2,1,0:T(8,128)S(1)} %bitcast.301, ...), kind=kLoop, calls=%fused_computation.169 | loop fusion | flops 9960704 | bytes 7349248 | tf_op jit(solution)/shard_map/transpose(jvp())/reduce_sum | solution.py:63
  93.3 6.1 %all-to-all-start = ((bf16[2,32,32,256]{3,2,0,1:T(8,128)(2,1)}), bf16[2,32,32,256]{3,2,0,1:T(8,128)(2,1)}, u32[]{:S(2)}, u32[]{:S(2)}) async-start(bf16[2,32,32,256]{3,2,0,1:T(8,128)(2,1)} %copy.36), calls=%async_computation | async-start | bytes 2097152 | tf_op jit(solution)/shard_map/all_to_all | solution.py:136
  99.4 3.0 %multiply_reduce_fusion = (f32[256]{0:T(256)}, f32[2,256]{1,0:T(2,128)S(1)}) fusion(f32[2,32,32,256]{3,2,1,0:T(8,128)} %get-tuple-element.38, f32[2,32,32,256]{3,2,1,0:T(8,128)S(1)} %get-tuple-element.40, f32[2,256]{1,0:T(2,128)S(1)} %fusion.22, f32[2,256]{1,0:T(2,128)S(1)} %fusion.23, f32[2,256]{1,0:T(2,128)S(1)} %fusion.21, f32[256]{0:T(256)S(1)} %copy-done.17), kind=kLoop, calls=%fused_computation.17 | loop fusion | flops 5242112 | bytes 4204544 | tf_op jit(solution)/shard_map/transpose(jvp())/reduce_sum | solution.py:63
  111.0 11.2 %all-to-all-done = bf16[2,32,32,256]{3,2,0,1:T(8,128)(2,1)} async-done(((bf16[2,32,32,256]{3,2,0,1:T(8,128)(2,1)}), bf16[2,32,32,256]{3,2,0,1:T(8,128)(2,1)}, u32[]{:S(2)}, u32[]{:S(2)}) %all-to-all-start) | async-done | bytes 1048608 | tf_op jit(solution)/shard_map/all_to_all | solution.py:136
  124.5 1.5 add_convert_fusion.2
  126.0 6.2 %all-to-all-start.1 = ((bf16[32,2,32,256]{3,2,1,0:T(8,128)(2,1)}), bf16[32,2,32,256]{3,2,1,0:T(8,128)(2,1)}, u32[]{:S(2)}, u32[]{:S(2)}) async-start(bf16[32,2,32,256]{3,2,1,0:T(8,128)(2,1)} %add_convert_fusion.2), calls=%async_computation.1 | async-start | bytes 2097152 | tf_op jit(solution)/shard_map/all_to_all | solution.py:141
  132.3 2.1 pad_maximum_fusion
  135.6 2.0 convolution_bitcast_fusion.2
  138.6 43.5 %all-reduce.11 = (f32[256]{0:T(256)}, f32[256]{0:T(256)}) all-reduce(f32[256]{0:T(256)S(1)} %copy-done.19, f32[256]{0:T(256)S(1)} %copy-done.18), channel_id=1, replica_groups=mesh['clip'=2,'tm'=16] {'clip','tm'}, use_global_device_ids=true, to_apply=%region_6.7 | all-reduce | flops 512 | bytes 4096 | tf_op jit(solution)/shard_map/psum | solution.py:169
  182.1 94.6 %all-reduce.15.cloned.1.call-done = (f32[3,3,128,256]{2,3,1,0:T(8,128)}, f32[3,256,256]{2,1,0:T(8,128)}) async-done(((f32[3,3,128,256]{2,3,1,0:T(8,128)}, f32[3,256,256]{2,1,0:T(8,128)}), (f32[3,3,128,256]{2,3,1,0:T(8,128)}, f32[3,256,256]{2,1,0:T(8,128)})) %all-reduce.15.cloned.1.call-update) | async-done | bytes 1966096 | tf_op jit(solution)/shard_map/psum | solution.py:169
  276.7 2.7 copy.44
  279.4 2.3 copy.39
  (135 shorter events, 38.8 us)
Async XLA Ops:
  7.2 10.8 %copy-start.8 = (bf16[1,2,64,64,128]{4,3,2,1,0:T(8,128)(2,1)S(1)}, bf16[1,2,64,64,128]{4,3,2,1,0:T(8,128)(2,1)}, u32[]{:S(2)}) copy-start(bf16[1,2,64,64,128]{4,3,2,1,0:T(8,128)(2,1)} %param.6) | copy-start | bytes 6291460
  9.6 32.9 %all-to-all-start.2 = ((bf16[2,32,32,256]{3,2,0,1:T(8,128)(2,1)}), bf16[2,32,32,256]{3,2,0,1:T(8,128)(2,1)}, u32[]{:S(2)}, u32[]{:S(2)}) async-start(bf16[2,32,32,256]{3,2,0,1:T(8,128)(2,1)} %bitcast.267), calls=%async_computation.2 | async-start | bytes 2097152 | tf_op jit(solution)/shard_map/all_to_all | solution.py:137
  18.0 4.6 %copy-start.16 = (bf16[3,3,128,256]{3,2,1,0:T(8,128)(2,1)S(1)}, bf16[3,3,128,256]{3,2,1,0:T(8,128)(2,1)}, u32[]{:S(2)}) copy-start(bf16[3,3,128,256]{3,2,1,0:T(8,128)(2,1)} %param.7) | copy-start | bytes 1769476
  23.4 46.5 %copy-start.23 = (s32[256]{0:T(256)}, s32[256]{0:T(256)S(1)}, u32[]{:S(2)}) copy-start(s32[256]{0:T(256)S(1)} %get-tuple-element.53) | copy-start | bytes 3076
  23.4 67.5 %copy-start.21 = (s32[256]{0:T(256)}, s32[256]{0:T(256)S(1)}, u32[]{:S(2)}) copy-start(s32[256]{0:T(256)S(1)} %get-tuple-element.52) | copy-start | bytes 3076
  23.5 4.2 %copy-start.5 = (bf16[2,32,1,32,1,128]{5,3,4,2,1,0:T(8,128)(2,1)}, bf16[2,32,1,32,1,128]{5,3,4,2,1,0:T(8,128)(2,1)S(1)}, u32[]{:S(2)}) copy-start(bf16[2,32,1,32,1,128]{5,3,4,2,1,0:T(8,128)(2,1)S(1)} %copy.55) | copy-start | bytes 1572868
  23.6 4.5 %copy-start.3 = (bf16[2,32,1,32,1,128]{5,3,4,2,1,0:T(8,128)(2,1)}, bf16[2,32,1,32,1,128]{5,3,4,2,1,0:T(8,128)(2,1)S(1)}, u32[]{:S(2)}) copy-start(bf16[2,32,1,32,1,128]{5,3,4,2,1,0:T(8,128)(2,1)S(1)} %copy.56) | copy-start | bytes 1572868
  23.7 40.8 %copy-start = (bf16[2,32,1,32,1,128]{5,3,1,0,4,2:T(8,128)(2,1)}, bf16[2,32,1,32,1,128]{5,3,1,0,4,2:T(8,128)(2,1)S(1)}, u32[]{:S(2)}) copy-start(bf16[2,32,1,32,1,128]{5,3,1,0,4,2:T(8,128)(2,1)S(1)} %copy.57) | copy-start | bytes 1572868
  56.5 28.9 %all-to-all-start.3 = ((bf16[16,2,2,32,256]{4,3,2,1,0:T(8,128)(2,1)}), bf16[16,2,2,32,256]{4,3,2,1,0:T(8,128)(2,1)}, u32[]{:S(2)}, u32[]{:S(2)}) async-start(bf16[16,2,2,32,256]{4,3,2,1,0:T(8,128)(2,1)} %fusion.30), calls=%async_computation.3 | async-start | bytes 2097152 | tf_op jit(solution)/shard_map/all_to_all | solution.py:143
  62.4 7.4 %copy-start.26 = (pred[256]{0:T(512)(128)(4,1)}, pred[256]{0:T(512)(128)(4,1)S(1)}, u32[]{:S(2)}) copy-start(pred[256]{0:T(512)(128)(4,1)S(1)} %compare_and_fusion) | copy-start | bytes 772
  62.4 2.2 copy-start.7
  64.6 2.3 copy-start.10
  87.6 3.3 %copy-start.24 = (s32[256]{0:T(256)S(1)}, s32[256]{0:T(256)}, u32[]{:S(2)}) copy-start(s32[256]{0:T(256)} %copy-done.23) | copy-start | bytes 3076
  87.6 3.3 %copy-start.27 = (pred[256]{0:T(512)(128)(4,1)S(1)}, pred[256]{0:T(512)(128)(4,1)}, u32[]{:S(2)}) copy-start(pred[256]{0:T(512)(128)(4,1)} %copy-done.26) | copy-start | bytes 772
  87.6 3.3 %copy-start.30 = (f32[2,32]{1,0:T(2,128)S(1)}, f32[2,32]{1,0:T(2,128)}, u32[]{:S(2)}) copy-start(f32[2,32]{1,0:T(2,128)} %copy-done.29) | copy-start | bytes 772
  93.3 28.9 %all-to-all-start = ((bf16[2,32,32,256]{3,2,0,1:T(8,128)(2,1)}), bf16[2,32,32,256]{3,2,0,1:T(8,128)(2,1)}, u32[]{:S(2)}, u32[]{:S(2)}) async-start(bf16[2,32,32,256]{3,2,0,1:T(8,128)(2,1)} %copy.36), calls=%async_computation | async-start | bytes 2097152 | tf_op jit(solution)/shard_map/all_to_all | solution.py:136
  99.3 3.1 %copy-start.22 = (s32[256]{0:T(256)S(1)}, s32[256]{0:T(256)}, u32[]{:S(2)}) copy-start(s32[256]{0:T(256)} %copy-done.21) | copy-start | bytes 3076
  99.3 3.1 %copy-start.25 = (s32[256]{0:T(256)S(1)}, s32[256]{0:T(256)}, u32[]{:S(2)}) copy-start(s32[256]{0:T(256)} %copy-done.23) | copy-start | bytes 3076
  99.4 3.0 %copy-start.28 = (pred[256]{0:T(512)(128)(4,1)S(1)}, pred[256]{0:T(512)(128)(4,1)}, u32[]{:S(2)}) copy-start(pred[256]{0:T(512)(128)(4,1)} %copy-done.26) | copy-start | bytes 772
  99.4 3.6 %copy-start.2 = (f32[2,32,32,256]{3,2,1,0:T(8,128)S(1)}, f32[2,32,32,256]{3,2,1,0:T(8,128)}, u32[]{:S(2)}) copy-start(f32[2,32,32,256]{3,2,1,0:T(8,128)} %get-tuple-element.38) | copy-start | bytes 6291460
  126.0 6.3 %copy-start.14 = (f32[1,3,128,256]{2,3,1,0:T(8,128)S(1)}, f32[1,3,128,256]{2,3,1,0:T(8,128)}, u32[]{:S(2)}) copy-start(f32[1,3,128,256]{2,3,1,0:T(8,128)} %maximum_bitcast_fusion.1) | copy-start | bytes 1179652
  126.0 153.4 %all-to-all-start.1 = ((bf16[32,2,32,256]{3,2,1,0:T(8,128)(2,1)}), bf16[32,2,32,256]{3,2,1,0:T(8,128)(2,1)}, u32[]{:S(2)}, u32[]{:S(2)}) async-start(bf16[32,2,32,256]{3,2,1,0:T(8,128)(2,1)} %add_convert_fusion.2), calls=%async_computation.1 | async-start | bytes 2097152 | tf_op jit(solution)/shard_map/all_to_all | solution.py:141
  132.2 144.5 %all-reduce.15.cloned.1.call-start = ((), (), s32[]{:S(2)}) async-start(), calls=%async_computation.4 | async-start | bytes 3932160 | tf_op jit(solution)/shard_map/psum | solution.py:169
  276.7 5.0 %copy-start.15 = (f32[3,256,256]{2,1,0:T(8,128)S(1)}, f32[3,256,256]{2,1,0:T(8,128)}, u32[]{:S(2)}) copy-start(f32[3,256,256]{2,1,0:T(8,128)} %get-tuple-element.58) | copy-start | bytes 2359300
  (12 other events, 11.6 us)
Sparse Core Ops, SparseCore 0:
  139.0 137.5 all-reduce.14
